TPU v7x, 256 devices: a whole 4x4x8 slice. The times are simulated.
256 devices in a mesh: frame: 8 (over x, y_lo), pos: 32 (over z, y_hi, core).
Axes of the slice: x: 4, y: 4 (y_hi: 2, y_lo: 2; y = y_hi * 2 + y_lo), z: 8, core: 2. Of those that a mesh axis runs over, the one named last changes fastest.
Arguments:
- frames_in: bfloat16 [512, 256, 512], P('frame', 'pos'), may hold values from -40 to 40
- attn_gain: float32 [512], replicated, may hold values from 0.5 to 1.5
- w_query: bfloat16 [512, 512], replicated, may hold values from -4 to 4
- w_key: bfloat16 [512, 512], replicated, may hold values from -4 to 4
- w_value: bfloat16 [512, 512], replicated, may hold values from -0.25 to 0.25
- w_output: bfloat16 [512, 512], replicated, may hold values from -0.25 to 0.25
- moe_gain: float32 [512], replicated, may hold values from 0.5 to 1.5
- dispatch_keys: bfloat16 [512, 1024], replicated, may hold values from -10 to 10
- w_in: bfloat16 [32, 512, 1024], P('pos'), may hold values from -0.25 to 0.25
- w_out: bfloat16 [32, 1024, 512], P('pos'), may hold values from -0.125 to 0.125
Outputs:
- frames_out: bfloat16 [512, 256, 512], P('frame', 'pos')
All inputs are finite; a program needn't handle non-finite values.
Results may differ from a plain program's by a relative error of at most 0.0052.
Values may be sent and summed in bfloat16 or wider, within the bound.
No kernel may reach another device: no remote copies, remote signals or barrier semaphores. Data moves between devices by JAX's collectives and lax.ppermute only.
A program may use at most 64 MiB of HBM per device.

v0:
```python
import jax
import jax.numpy as jnp
from jax import lax
from jax.sharding import PartitionSpec as P

HEADS = 8
EXPERTS = 16
SLOTS = 64
EPS = 1e-06
LOGIT_SCALE = 3.0
MASKED = -1e30


def copy_for_each(shard, axis):
    copies = jnp.broadcast_to(shard, (lax.axis_size(axis), *shard.shape))
    return lax.all_to_all(copies, axis, split_axis=0, concat_axis=0, tiled=True)


def collected_together(shard, axis):
    leaves = jax.tree.leaves(shard)
    sequence = sorted(range(len(leaves)), key=lambda k: -leaves[k].size)
    width = (1, *leaves[sequence[0]].shape)[-1]
    lines = [
        jnp.pad(leaves[k].reshape(-1), (0, -leaves[k].size % width)).reshape(-1, width)
        for k in sequence
    ]
    both, at, found = (copy_for_each(jnp.concatenate(lines), axis), 0, {})
    for k, line in zip(sequence, lines):
        piece = both[:, at : at + len(line)].reshape(len(both), -1)
        found[k] = piece[:, : leaves[k].size].reshape(-1, *leaves[k].shape)
        at += len(line)
    numbers = iter(range(len(leaves)))
    return jax.tree.map(lambda _: found[next(numbers)], shard)


def combined_pairwise(pieces, combine):
    while len(jax.tree.leaves(pieces)[0]) > 1:
        pieces = jax.vmap(combine)(
            *(jax.tree.map(lambda part: part[side::2], pieces) for side in (0, 1))
        )
    return jax.tree.map(lambda part: part[0], pieces)


def merged(shard, axis, combine):
    pieces = collected_together(shard, axis)
    return combined_pairwise(pieces, combine)


def in_blocks(shard, dim, length):
    before, after = (shard.shape[:dim], shard.shape[dim + 1 :])
    return jnp.moveaxis(shard.reshape(*before, length, -1, *after), dim, 0)


def sum_at_owner(shard, axis, dim):
    length = lax.axis_size(axis)
    blocks = lax.all_to_all(in_blocks(shard, dim, length), axis, 0, 0, tiled=True)
    return jnp.sum(blocks.astype(jnp.float32), axis=0)


def from_partner(block, axis, apart):
    count = lax.axis_size(axis)
    route = []
    for low in range(count):
        high = low | 1 << apart
        if high != low and high < count:
            route += [(low, high), (high, low)]
    return lax.ppermute(block, axis, route)


def in_order(blocks, dim):
    blocks = jnp.moveaxis(blocks, 0, dim)
    dims = blocks.shape
    return blocks.reshape(*dims[:dim], dims[dim] * dims[dim + 1], *dims[dim + 2 :])


def collect(shard, axis, dim):
    return in_order(copy_for_each(shard, axis), dim)


def rms_scale(values_in, gain):
    values_in = values_in.astype(jnp.float32)
    mean_sq = jnp.mean(values_in * values_in, axis=-1, keepdims=True)
    return values_in * lax.rsqrt(mean_sq + EPS) * gain


def project(rows_in, weights):
    return jnp.dot(rows_in, weights, preferred_element_type=jnp.float32).astype(jnp.bfloat16)


def softmax_rows(scores, axis_index):
    largest = jnp.max(scores, axis=axis_index, keepdims=True)
    weights = jnp.exp(scores - largest)
    return (weights / jnp.sum(weights, axis=axis_index, keepdims=True)).astype(jnp.bfloat16)


def attend(queries, keys_block, values_block):
    frame_count = queries.shape[0]
    score_scale = queries.shape[3] ** (-0.5)
    causal = jnp.arange(frame_count)[:, None] >= jnp.arange(frame_count)[None, :]

    def one_head(triple):
        queries_head, keys_head, values_head = triple
        scores = (
            jnp.einsum("fpd,gpd->pfg", queries_head, keys_head, preferred_element_type=jnp.float32)
            * score_scale
        )
        scores = jnp.where(causal[None], scores, MASKED)
        attention = softmax_rows(scores, 2)
        return jnp.einsum(
            "pfg,gpd->fpd", attention, values_head, preferred_element_type=jnp.float32
        ).astype(jnp.bfloat16)

    by_head = tuple(
        (jnp.moveaxis(array_in, 2, 0) for array_in in (queries, keys_block, values_block))
    )
    return jnp.moveaxis(lax.map(one_head, by_head), 0, 2)


def merge_stats(first_pair, second_pair):
    largest = jnp.maximum(first_pair[0], second_pair[0])
    totals = first_pair[1] * jnp.exp(first_pair[0] - largest) + second_pair[1] * jnp.exp(
        second_pair[0] - largest
    )
    return (largest, totals)


def local(
    frames_in, attn_gain, w_query, w_key, w_value, w_output, moe_gain, dispatch_keys, w_in, w_out
):
    frame_count, pos_count, features = frames_in.shape
    head_dim = features // HEADS
    normed = rms_scale(frames_in, attn_gain).astype(jnp.bfloat16)
    spread = lax.all_to_all(normed, "frame", split_axis=1, concat_axis=0, tiled=True)
    all_frames = spread.shape[0]
    pos_part = spread.shape[1]
    flattened = spread.reshape(all_frames * pos_part, features)
    shaped = (all_frames, pos_part, HEADS, head_dim)
    queries = project(flattened, w_query).reshape(shaped)
    keys_block = project(flattened, w_key).reshape(shaped)
    values_block = project(flattened, w_value).reshape(shaped)
    mixed_part = attend(queries, keys_block, values_block).reshape(all_frames, pos_part, features)
    mixed_heads = lax.all_to_all(mixed_part, "frame", split_axis=0, concat_axis=1, tiled=True)
    mixed_heads = mixed_heads.reshape(frame_count * pos_count, features)
    residual = (
        frames_in.reshape(frame_count * pos_count, features).astype(jnp.float32)
        + jnp.dot(mixed_heads, w_output, preferred_element_type=jnp.float32)
    ).astype(jnp.bfloat16)
    moe_input = rms_scale(residual, moe_gain).astype(jnp.bfloat16)
    logits = LOGIT_SCALE * jnp.dot(moe_input, dispatch_keys, preferred_element_type=jnp.float32)
    local_max = jnp.max(logits, axis=0)
    local_sum = jnp.sum(jnp.exp(logits - local_max[None, :]), axis=0)
    largest, totals = merged((local_max, local_sum), "pos", merge_stats)
    dispatch = (jnp.exp(logits - largest[None, :]) / totals[None, :]).astype(jnp.bfloat16)
    count_pos = lax.axis_size("pos")
    position = lax.axis_index("pos")
    splits = max(1, count_pos // EXPERTS)
    split_bits = splits.bit_length() - 1
    pieces_dev = EXPERTS * splits // count_pos
    local_experts = max(1, pieces_dev // splits)
    columns = dispatch
    slot_in = sum_at_owner(
        lax.dot_general(
            columns, moe_input, (((0,), (0,)), ((), ())), preferred_element_type=jnp.float32
        ).astype(jnp.bfloat16),
        "pos",
        0,
    ).astype(jnp.bfloat16)
    bit_index = 0
    partner = from_partner(slot_in, "pos", bit_index)
    upper_bit = position // 2**bit_index % 2 == 1
    slot_in = jnp.where(
        upper_bit,
        jnp.concatenate([partner, slot_in], axis=0),
        jnp.concatenate([slot_in, partner], axis=0),
    )
    slot_in = slot_in.reshape(local_experts, SLOTS, features)
    hidden = jax.nn.gelu(
        jnp.einsum("esd,edh->esh", slot_in, w_in, preferred_element_type=jnp.float32)
    ).astype(jnp.bfloat16)
    partial_out = jnp.einsum(
        "esh,ehd->esd", hidden, w_out, preferred_element_type=jnp.float32
    ).astype(jnp.bfloat16)
    shares = partial_out.astype(jnp.float32).reshape(pieces_dev * SLOTS, features)
    for bit_index in reversed(range(split_bits)):
        half_rows = shares.shape[0] // 2
        lower_half = shares[:half_rows]
        upper_half = shares[half_rows:]
        upper_bit = position // 2**bit_index % 2 == 1
        kept_rows = jnp.where(upper_bit, upper_half, lower_half)
        sent_rows = jnp.where(upper_bit, lower_half, upper_half)
        shares = kept_rows + from_partner(sent_rows.astype(jnp.bfloat16), "pos", bit_index).astype(
            sent_rows.dtype
        )
    outputs = shares.astype(jnp.bfloat16)
    combine = softmax_rows(logits, 1)
    columns = combine
    moe_out = jnp.dot(columns, collect(outputs, "pos", 0), preferred_element_type=jnp.float32)
    frames_out = (residual.astype(jnp.float32) + moe_out).astype(jnp.bfloat16)
    return frames_out.reshape(frame_count, pos_count, features)


def solution(mesh):
    in_specs = (
        P("frame", "pos", None),
        P(),
        P(),
        P(),
        P(),
        P(),
        P(),
        P(),
        P("pos", None, None),
        P("pos", None, None),
    )
    out_specs = P("frame", "pos", None)
    return jax.shard_map(local, mesh=mesh, in_specs=in_specs, out_specs=out_specs, check_vma=False)
```

profile of v0, /device:TPU:1, one launch (start us, length us, event | category | flops | bytes accessed | tf_op | source)
XLA Modules:
  0.0 160.5 jit_solution(891300015364039977)
XLA Ops:
  0.0 1.4 multiply_reduce_fusion
  1.5 2.1 %multiply_convert_fusion = bf16[64,8,512]{2,0,1:T(8,128)(2,1)} fusion(f32[512]{0:T(512)} %param.13, f32[64,8]{0,1:T(8,128)S(1)} %add_rsqrt_fusion, bf16[64,8,512]{2,1,0:T(8,128)(2,1)} %param.12), kind=kLoop, calls=%fused_computation.44 | loop fusion | flops 1048576 | bytes 1052672 | tf_op jit(solution)/shard_map/convert_element_type | solution.py:132
  3.5 6.0 %all-to-all-start = ((bf16[64,8,512]{2,0,1:T(8,128)(2,1)}), bf16[64,8,512]{2,0,1:T(8,128)(2,1)S(1)}, u32[]{:S(2)}, u32[]{:S(2)}) async-start(bf16[64,8,512]{2,0,1:T(8,128)(2,1)} %multiply_convert_fusion), calls=%async_computation | async-start | bytes 1048576 | tf_op jit(solution)/shard_map/all_to_all | solution.py:133
  9.5 8.7 %all-to-all-done = bf16[64,8,512]{2,0,1:T(8,128)(2,1)S(1)} async-done(((bf16[64,8,512]{2,0,1:T(8,128)(2,1)}), bf16[64,8,512]{2,0,1:T(8,128)(2,1)S(1)}, u32[]{:S(2)}, u32[]{:S(2)}) %all-to-all-start) | async-done | bytes 524320 | tf_op jit(solution)/shard_map/all_to_all | solution.py:133
  18.2 1.3 convolution_convert_fusion.3
  19.5 0.5 convolution_convert_fusion.2
  20.0 0.5 convolution_convert_fusion.4
  20.5 18.8 %while.11 = (s32[]{:T(128)}, bf16[8,512,1,64]{1,3,2,0:T(8,128)(2,1)}, bf16[8,512,1,64]{1,3,2,0:T(8,128)(2,1)S(1)}, bf16[8,512,1,64]{1,3,2,0:T(8,128)(2,1)}, bf16[8,512,1,64]{1,3,2,0:T(8,128)(2,1)S(1)}, /*index=5*/s32[]{:T(128)}) while((s32[]{:T(128)}, bf16[8,512,1,64]{1,3,2,0:T(8,128)(2,1)}, bf16[8,512,1,64]{1,3,2,0:T(8,128)(2,1)S(1)}, ...), condition=%wide.region_4.5_spmd.clone, body=%wide.region_1.4_spmd.clone.sunk | while | flops 69499904 | bytes 3420229 | solution.py:116
  20.5 1.2 fusion.86
  21.7 0.2 fusion.87
  21.9 0.9 fusion.88
  22.9 1.2 fusion.86
  24.1 0.2 fusion.87
  24.3 0.9 fusion.88
  25.2 1.2 fusion.86
  26.6 0.9 fusion.88
  27.6 1.2 fusion.86
  29.0 0.9 fusion.88
  29.9 1.2 fusion.86
  31.3 1.0 fusion.88
  32.3 1.2 fusion.86
  33.6 0.9 fusion.88
  34.6 1.2 fusion.86
  36.0 0.9 fusion.88
  37.0 1.2 fusion.86
  38.3 0.9 fusion.88
  39.3 0.5 broadcast.50
  39.8 2.0 %reduce.5 = bf16[512,512]{0,1:T(8,128)(2,1)S(1)} reduce(bf16[512,1,512]{0,2,1:T(8,128)(2,1)} %bitcast.117, bf16[]{:T(256)} %broadcast.50), dimensions={1}, to_apply=%copy.38.reduce_sub_computation | reduce | bytes 1048578 | tf_op jit(solution)/shard_map/reshape | solution.py:141
  41.9 0.2 copy.58
  42.1 1.2 reshape.156
  43.2 3.7 %all-to-all-start.1 = ((bf16[8,2,16384]{2,1,0:T(2,128)(2,1)}), bf16[8,2,16384]{2,1,0:T(2,128)(2,1)S(1)}, u32[]{:S(2)}, u32[]{:S(2)}) async-start(bf16[8,2,16384]{2,1,0:T(2,128)(2,1)} %reshape.156), calls=%async_computation.1 | async-start | bytes 1048576 | tf_op jit(solution)/shard_map/all_to_all | solution.py:142
  46.9 1.2 copy_convert_fusion
  48.1 6.9 %all-to-all-done.1 = bf16[8,2,16384]{2,1,0:T(2,128)(2,1)S(1)} async-done(((bf16[8,2,16384]{2,1,0:T(2,128)(2,1)}), bf16[8,2,16384]{2,1,0:T(2,128)(2,1)S(1)}, u32[]{:S(2)}, u32[]{:S(2)}) %all-to-all-start.1) | async-done | bytes 524320 | tf_op jit(solution)/shard_map/all_to_all | solution.py:142
  55.0 0.5 reshape.157
  55.7 2.2 %fusion.20 = (f32[512]{0:T(512)S(1)}, bf16[512,512]{1,0:T(8,128)(2,1)S(1)}) fusion(bf16[512,512]{1,0:T(8,128)(2,1)S(1)} %copy-done.8, bf16[64,8,1,512]{3,0,1,2:T(8,128)(2,1)S(1)} %bitcast.116, f32[64,8,512]{2,0,1:T(8,128)} %copy_convert_fusion), kind=kOutput, calls=%fused_computation.38 | convolution fusion | flops 269745664 | bytes 2623488 | tf_op jit(solution)/shard_map/dot_general | solution.py:146
  58.0 0.9 fusion.69
  58.9 0.7 fusion.14
  59.7 26.0 %all_to_all.45 = f32[32,2,1024]{2,1,0:T(2,128)S(1)} all-to-all(f32[32,2,1024]{2,1,0:T(2,128)S(1)} %broadcast_in_dim.18), channel_id=1, replica_groups=mesh['frame'=8,'pos'=32] {'pos'}, dimensions={0} | all-to-all | bytes 524288 | tf_op jit(solution)/shard_map/all_to_all | solution.py:16
  85.7 0.2 fusion.71
  86.5 1.9 %convolution_convert_fusion.1 = bf16[1024,512]{1,0:T(8,128)(2,1)S(1)} fusion(f32[512,1024]{1,0:T(8,128)S(1)} %get-tuple-element.80, f32[1024]{0:T(1024)S(1)} %bitcast.120, f32[1024]{0:T(1024)S(1)} %bitcast.121, bf16[512,512]{1,0:T(8,128)(2,1)} %copy-done.10, f32[512]{0:T(512)S(1)} %copy-done.9, f32[512]{0:T(512)S(1)} %add_rsqrt_fusion.1), kind=kOutput, calls=%fused_computation.27 | convolution fusion | flops 540016640 | bytes 3682304 | tf_op jit(solution)/shard_map/dot_general | solution.py:162
  88.4 32.1 %all_to_all.46 = bf16[32,32,512]{2,1,0:T(8,128)(2,1)S(1)} all-to-all(bf16[32,32,512]{2,1,0:T(8,128)(2,1)S(1)} %bitcast.112), channel_id=1, replica_groups=mesh['frame'=8,'pos'=32] {'pos'}, dimensions={0} | all-to-all | bytes 2097152 | tf_op jit(solution)/shard_map/all_to_all | solution.py:56
  120.7 0.8 collective-permute-start
  121.5 0.9 collective-permute-done
  122.4 1.7 %fusion.19 = f32[1,64,512]{2,1,0:T(8,128)S(1)} fusion(bf16[1,1024,512]{2,1,0:T(8,128)(2,1)S(1)} %copy-done.4, bf16[1,512,1024]{2,1,0:T(8,128)(2,1)} %param.20, bf16[32,512]{1,0:T(8,128)(2,1)S(1)} %reduce_sum.61, bf16[32,512]{1,0:T(8,128)(2,1)S(1)} %collective-permute-done, pred[]{:T(512)S(6)} %eq.7), kind=kOutput, calls=%fused_computation.37 | convolution fusion | flops 135168000 | bytes 2293761 | tf_op jit(solution)/shard_map/esh,ehd->esd/dot_general | solution.py:180
  124.2 0.4 collective-permute-start.1
  124.6 0.9 collective-permute-done.1
  125.6 33.3 %all_to_all.47 = bf16[32,32,512]{2,1,0:T(8,128)(2,1)S(1)} all-to-all(bf16[32,32,512]{2,1,0:T(8,128)(2,1)S(1)} %broadcast_in_dim.19), channel_id=1, replica_groups=mesh['frame'=8,'pos'=32] {'pos'}, dimensions={0} | all-to-all | bytes 2097152 | tf_op jit(solution)/shard_map/all_to_all | solution.py:16
  158.9 1.6 fusion.17
  (62 shorter events, 2.3 us)
Async XLA Ops:
  0.0 58.0 %copy-start = (bf16[512,1024]{1,0:T(8,128)(2,1)S(1)}, bf16[512,1024]{1,0:T(8,128)(2,1)}, u32[]{:S(2)}) copy-start(bf16[512,1024]{1,0:T(8,128)(2,1)} %param.19) | copy-start | bytes 3145732
  0.0 18.2 %copy-start.5 = (bf16[512,512]{1,0:T(8,128)(2,1)S(1)}, bf16[512,512]{1,0:T(8,128)(2,1)}, u32[]{:S(2)}) copy-start(bf16[512,512]{1,0:T(8,128)(2,1)} %param.14) | copy-start | bytes 1572868
  0.0 19.5 %copy-start.6 = (bf16[512,512]{1,0:T(8,128)(2,1)S(1)}, bf16[512,512]{1,0:T(8,128)(2,1)}, u32[]{:S(2)}) copy-start(bf16[512,512]{1,0:T(8,128)(2,1)} %param.15) | copy-start | bytes 1572868
  3.5 16.5 %copy-start.7 = (bf16[512,512]{1,0:T(8,128)(2,1)S(1)}, bf16[512,512]{1,0:T(8,128)(2,1)}, u32[]{:S(2)}) copy-start(bf16[512,512]{1,0:T(8,128)(2,1)} %param.16) | copy-start | bytes 1572868
  3.5 14.7 %all-to-all-start = ((bf16[64,8,512]{2,0,1:T(8,128)(2,1)}), bf16[64,8,512]{2,0,1:T(8,128)(2,1)S(1)}, u32[]{:S(2)}, u32[]{:S(2)}) async-start(bf16[64,8,512]{2,0,1:T(8,128)(2,1)} %multiply_convert_fusion), calls=%async_computation | async-start | bytes 1048576 | tf_op jit(solution)/shard_map/all_to_all | solution.py:133
  39.8 7.1 %copy-start.1 = (bf16[64,8,512]{2,1,0:T(8,128)(2,1)S(1)}, bf16[64,8,512]{2,1,0:T(8,128)(2,1)}, u32[]{:S(2)}) copy-start(bf16[64,8,512]{2,1,0:T(8,128)(2,1)} %param.12) | copy-start | bytes 1572868
  43.2 11.8 %all-to-all-start.1 = ((bf16[8,2,16384]{2,1,0:T(2,128)(2,1)}), bf16[8,2,16384]{2,1,0:T(2,128)(2,1)S(1)}, u32[]{:S(2)}, u32[]{:S(2)}) async-start(bf16[8,2,16384]{2,1,0:T(2,128)(2,1)} %reshape.156), calls=%async_computation.1 | async-start | bytes 1048576 | tf_op jit(solution)/shard_map/all_to_all | solution.py:142
  48.1 7.6 %copy-start.8 = (bf16[512,512]{1,0:T(8,128)(2,1)S(1)}, bf16[512,512]{1,0:T(8,128)(2,1)}, u32[]{:S(2)}) copy-start(bf16[512,512]{1,0:T(8,128)(2,1)} %param.17) | copy-start | bytes 1572868
  55.6 2.4 %copy-start.9 = (f32[512]{0:T(512)S(1)}, f32[512]{0:T(512)}, u32[]{:S(2)}) copy-start(f32[512]{0:T(512)} %param.18) | copy-start | bytes 6148
  57.9 0.9 copy-start.10
  58.9 27.7 %copy-start.2 = (f32[512,1024]{1,0:T(8,128)}, f32[512,1024]{1,0:T(8,128)S(1)}, u32[]{:S(2)}) copy-start(f32[512,1024]{1,0:T(8,128)S(1)} %get-tuple-element.80) | copy-start | bytes 6291460
  88.4 34.0 %copy-start.4 = (bf16[1,1024,512]{2,1,0:T(8,128)(2,1)S(1)}, bf16[1,1024,512]{2,1,0:T(8,128)(2,1)}, u32[]{:S(2)}) copy-start(bf16[1,1024,512]{2,1,0:T(8,128)(2,1)} %param.21) | copy-start | bytes 3145732
  120.7 1.7 %collective-permute-start = (bf16[32,512]{1,0:T(8,128)(2,1)S(1)}, bf16[32,512]{1,0:T(8,128)(2,1)S(1)}, u32[]{:S(2)}, u32[]{:S(2)}) collective-permute-start(bf16[32,512]{1,0:T(8,128)(2,1)S(1)} %reduce_sum.61), channel_id=1, source_target_pairs={{0,1},{1,0},{2,3},{3,2},{4,5},{5,4},{6,7},{7,6},{8,9},{9,8},{10,11... | collective-permute-start | bytes 98312 | tf_op jit(solution)/shard_map/ppermute | solution.py:67
  124.1 34.8 %copy-start.3 = (f32[512,1024]{1,0:T(8,128)S(1)}, f32[512,1024]{1,0:T(8,128)}, u32[]{:S(2)}) copy-start(f32[512,1024]{1,0:T(8,128)} %copy-done.2) | copy-start | bytes 6291460
  124.2 34.8 %copy-start.11 = (bf16[512,512]{1,0:T(8,128)(2,1)S(1)}, bf16[512,512]{1,0:T(8,128)(2,1)}, u32[]{:S(2)}) copy-start(bf16[512,512]{1,0:T(8,128)(2,1)} %copy-done.10) | copy-start | bytes 1572868
  124.2 1.3 collective-permute-start.1
where the time goes:
time: 161 us
  blocking collectives  91.4 us (57%)
  matrix products  27.7 us (17%)
  waiting for transfers between devices  17.4 us (11%)
  starting transfers between devices  10.9 us (7%)
  other arithmetic  9.34 us (6%)
  local copies, waits for them, and re-layouts  3.4 us (2%)
    all_to_all x2, blocking collectives, copy_for_each(): return lax.all_to_all(copies, axis, split_axis=0, concat_axis=0, tiled=True)  59.3 us
    all_to_all x1, blocking collectives, sum_at_owner(): lax.all_to_all(in_blocks(shard, dim, length), axis, 0, 0, tiled=True)  32.1 us
    dot_general x8, matrix products, one_head(): jnp.einsum('fpd,gpd->pfg', queries_head, keys_head, preferred_element_typ...  9.6 us
    all_to_all x1, waiting for transfers between devices, local(): lax.all_to_all(normed, 'frame', split_axis=1, concat_axis=0, tiled=True)  8.71 us
    dot_general x8, matrix products, one_head(): jnp.einsum('pfg,gpd->fpd', attention, values_head, preferred_element_type...  7.6 us
    all_to_all x1, waiting for transfers between devices, local(): lax.all_to_all(mixed_part, 'frame', split_axis=0, concat_axis=1, tiled=True)  6.94 us
    all_to_all x1, starting transfers between devices, local(): lax.all_to_all(normed, 'frame', split_axis=1, concat_axis=0, tiled=True)  5.98 us
    all_to_all x1, starting transfers between devices, local(): lax.all_to_all(mixed_part, 'frame', split_axis=0, concat_axis=1, tiled=True)  3.67 us
  transfers between devices with their start and end apart: 4, of which 4 were waited for; matrix products, arithmetic and copies ran while one was open for 1% of the time, Pallas kernels for 0%

commit v1 on v0

--- a/solution.py
+++ b/solution.py
@@ -139,7 +139,12 @@
     keys_block = project(flattened, w_key).reshape(shaped)
     values_block = project(flattened, w_value).reshape(shaped)
     mixed_part = attend(queries, keys_block, values_block).reshape(all_frames, pos_part, features)
-    mixed_heads = lax.all_to_all(mixed_part, "frame", split_axis=0, concat_axis=1, tiled=True)
+    mixed_heads = jnp.concatenate(
+        lax.all_to_all(
+            jnp.stack(jnp.split(mixed_part, lax.axis_size("frame"), axis=0)), "frame", 0, 0
+        ),
+        axis=1,
+    )
     mixed_heads = mixed_heads.reshape(frame_count * pos_count, features)
     residual = (
         frames_in.reshape(frame_count * pos_count, features).astype(jnp.float32)

time: 161 us -> 158 us (0.981)
  matrix products: 27.7 us -> 22.5 us
  local copies, waits for them, and re-layouts: 3.4 us -> 7.02 us
  other arithmetic: 9.34 us -> 6.32 us
    dot_general x8, matrix products: 7.6 us -> 2.5 us  [one_head(): jnp.einsum('pfg,gpd->fpd', attention, values_head, preferred_element_type...]
    unnamed x28 -> x29, local copies, waits for them, and re-layouts: 2.08 us -> 4.49 us
    reshape x1 -> x0, other arithmetic: 2.04 us -> none  [local(): attend(queries, keys_block, values_block)]
  transfers between devices with their start and end apart: 4 -> 4, of which waited for: 4 -> 4; matrix products, arithmetic and copies ran while one was open for 1% -> 0% of each run, Pallas kernels for 0% -> 0%
where the time goes in v1:
time: 158 us; the launch traced here: 157 us
  blocking collectives  91.4 us (58%)
  matrix products  22.5 us (14%)
  waiting for transfers between devices  18.3 us (12%)
  starting transfers between devices  10.8 us (7%)
  local copies, waits for them, and re-layouts  7.02 us (4%)
  other arithmetic  6.32 us (4%)
    all_to_all x2, blocking collectives, copy_for_each(): return lax.all_to_all(copies, axis, split_axis=0, concat_axis=0, tiled=True)  59.3 us
    all_to_all x1, blocking collectives, sum_at_owner(): lax.all_to_all(in_blocks(shard, dim, length), axis, 0, 0, tiled=True)  32.1 us
    dot_general x8, matrix products, one_head(): jnp.einsum('fpd,gpd->pfg', queries_head, keys_head, preferred_element_typ...  9.6 us
    all_to_all x1, waiting for transfers between devices, local(): lax.all_to_all(normed, 'frame', split_axis=1, concat_axis=0, tiled=True)  8.71 us
    all_to_all x1, waiting for transfers between devices, local(): lax.all_to_all(jnp.stack(jnp.split(mixed_part, lax.axis_size('frame'), ax...  7.92 us
    all_to_all x1, starting transfers between devices, local(): lax.all_to_all(normed, 'frame', split_axis=1, concat_axis=0, tiled=True)  5.85 us
    unnamed x29, local copies, waits for them, and re-layouts  4.49 us
    all_to_all x1, starting transfers between devices, local(): lax.all_to_all(jnp.stack(jnp.split(mixed_part, lax.axis_size('frame'), ax...  3.68 us
  transfers between devices with their start and end apart: 4, of which 4 were waited for; matrix products, arithmetic and copies ran while one was open for 0% of the time, Pallas kernels for 0%

profile of v1, /device:TPU:1, one launch (start us, length us, event | category | flops | bytes accessed | tf_op | source)
XLA Modules:
  0.0 156.8 jit_solution(13137158614427010459)
XLA Ops:
  0.0 1.4 multiply_reduce_fusion
  1.5 2.1 %multiply_convert_fusion = bf16[64,8,512]{2,0,1:T(8,128)(2,1)} fusion(f32[512]{0:T(512)} %param.13, f32[64,8]{0,1:T(8,128)S(1)} %add_rsqrt_fusion, bf16[64,8,512]{2,1,0:T(8,128)(2,1)} %param.12), kind=kLoop, calls=%fused_computation.44 | loop fusion | flops 1048576 | bytes 1052672 | tf_op jit(solution)/shard_map/convert_element_type | solution.py:132
  3.5 5.9 %all-to-all-start = ((bf16[64,8,512]{2,0,1:T(8,128)(2,1)}), bf16[64,8,512]{2,0,1:T(8,128)(2,1)S(1)}, u32[]{:S(2)}, u32[]{:S(2)}) async-start(bf16[64,8,512]{2,0,1:T(8,128)(2,1)} %multiply_convert_fusion), calls=%async_computation | async-start | bytes 1048576 | tf_op jit(solution)/shard_map/all_to_all | solution.py:133
  9.4 8.7 %all-to-all-done = bf16[64,8,512]{2,0,1:T(8,128)(2,1)S(1)} async-done(((bf16[64,8,512]{2,0,1:T(8,128)(2,1)}), bf16[64,8,512]{2,0,1:T(8,128)(2,1)S(1)}, u32[]{:S(2)}, u32[]{:S(2)}) %all-to-all-start) | async-done | bytes 524320 | tf_op jit(solution)/shard_map/all_to_all | solution.py:133
  18.1 1.3 convolution_convert_fusion.3
  19.4 0.5 convolution_convert_fusion.2
  19.9 0.5 convolution_convert_fusion.4
  20.4 13.8 %while.11 = (s32[]{:T(128)}, bf16[8,512,1,64]{1,3,2,0:T(8,128)(2,1)S(1)}, bf16[8,512,1,64]{1,3,2,0:T(8,128)(2,1)S(1)}, bf16[8,512,1,64]{1,3,2,0:T(8,128)(2,1)}, bf16[8,512,1,64]{1,3,2,0:T(8,128)(2,1)S(1)}, /*index=5*/s32[]{:T(128)}) while((s32[]{:T(128)}, bf16[8,512,1,64]{1,3,2,0:T(8,128)(2,1)S(1)}, ...), condition=%wide.region_4.5_spmd.clone, body=%wide.region_1.4_spmd.clone.sunk | while | flops 69499904 | bytes 3420229 | solution.py:116
  20.4 1.2 fusion.87
  21.8 0.3 fusion.89
  22.1 1.2 fusion.87
  23.5 0.3 fusion.89
  23.8 1.2 fusion.87
  25.2 0.3 fusion.89
  25.6 1.2 fusion.87
  27.0 0.3 fusion.89
  27.3 1.2 fusion.87
  28.7 0.3 fusion.89
  29.0 1.2 fusion.87
  30.4 0.3 fusion.89
  30.7 1.2 fusion.87
  32.1 0.3 fusion.89
  32.5 1.2 fusion.87
  33.9 0.3 fusion.89
  34.2 0.3 fusion.71
  34.6 0.6 constant_dynamic-update-slice_fusion.7
  36.0 0.6 constant_dynamic-update-slice_fusion.6
  36.6 0.6 constant_dynamic-update-slice_fusion.5
  37.3 0.6 constant_dynamic-update-slice_fusion.4
  37.9 0.6 constant_dynamic-update-slice_fusion.3
  38.5 0.6 constant_dynamic-update-slice_fusion.2
  39.2 0.6 constant_dynamic-update-slice_fusion.1
  39.8 0.6 constant_dynamic-update-slice_fusion
  40.4 3.7 %all-to-all-start.1 = ((bf16[8,64,1,512]{3,1,2,0:T(8,128)(2,1)}), bf16[8,64,1,512]{3,1,2,0:T(8,128)(2,1)S(1)}, u32[]{:S(2)}, u32[]{:S(2)}) async-start(bf16[8,64,1,512]{3,1,2,0:T(8,128)(2,1)} %constant_dynamic-update-slice_fusion), calls=%async_computation.1 | async-start | bytes 1048576 | tf_op jit(solution)/shard_map/all_to_all | solution.py:143
  44.3 7.9 %all-to-all-done.1 = bf16[8,64,1,512]{3,1,2,0:T(8,128)(2,1)S(1)} async-done(((bf16[8,64,1,512]{3,1,2,0:T(8,128)(2,1)}), bf16[8,64,1,512]{3,1,2,0:T(8,128)(2,1)S(1)}, u32[]{:S(2)}, u32[]{:S(2)}) %all-to-all-start.1) | async-done | bytes 524320 | tf_op jit(solution)/shard_map/all_to_all | solution.py:143
  52.2 2.1 %fusion.20 = (f32[512]{0:T(512)S(1)}, bf16[512,512]{1,0:T(8,128)(2,1)S(1)}) fusion(bf16[512,512]{1,0:T(8,128)(2,1)} %param.17, bf16[64,8,1,512]{3,0,2,1:T(8,128)(2,1)S(1)} %bitcast.127, f32[64,8,512]{2,0,1:T(8,128)S(1)} %copy_convert_fusion), kind=kOutput, calls=%fused_computation.38 | convolution fusion | flops 269745664 | bytes 2623488 | tf_op jit(solution)/shard_map/dot_general | solution.py:151
  54.3 0.9 fusion.69
  55.2 0.7 fusion.14
  56.0 26.0 %all_to_all.35 = f32[32,2,1024]{2,1,0:T(2,128)S(1)} all-to-all(f32[32,2,1024]{2,1,0:T(2,128)S(1)} %broadcast_in_dim.18), channel_id=1, replica_groups=mesh['frame'=8,'pos'=32] {'pos'}, dimensions={0} | all-to-all | bytes 524288 | tf_op jit(solution)/shard_map/all_to_all | solution.py:16
  82.9 1.9 %convolution_convert_fusion.1 = bf16[1024,512]{1,0:T(8,128)(2,1)S(1)} fusion(f32[512,1024]{1,0:T(8,128)S(1)} %get-tuple-element.88, f32[1024]{0:T(1024)S(1)} %bitcast.130, f32[1024]{0:T(1024)S(1)} %bitcast.131, bf16[512,512]{1,0:T(8,128)(2,1)} %copy-done.9, f32[512]{0:T(512)S(1)} %copy-done.8, f32[512]{0:T(512)S(1)} %add_rsqrt_fusion.1), kind=kOutput, calls=%fused_computation.27 | convolution fusion | flops 540016640 | bytes 3682304 | tf_op jit(solution)/shard_map/dot_general | solution.py:167
  84.8 32.1 %all_to_all.36 = bf16[32,32,512]{2,1,0:T(8,128)(2,1)S(1)} all-to-all(bf16[32,32,512]{2,1,0:T(8,128)(2,1)S(1)} %bitcast.115), channel_id=1, replica_groups=mesh['frame'=8,'pos'=32] {'pos'}, dimensions={0} | all-to-all | bytes 2097152 | tf_op jit(solution)/shard_map/all_to_all | solution.py:56
  117.0 0.8 collective-permute-start
  117.9 0.9 collective-permute-done
  118.7 1.7 %fusion.19 = f32[1,64,512]{2,1,0:T(8,128)S(1)} fusion(bf16[1,1024,512]{2,1,0:T(8,128)(2,1)S(1)} %copy-done.4, bf16[1,512,1024]{2,1,0:T(8,128)(2,1)} %param.20, bf16[32,512]{1,0:T(8,128)(2,1)S(1)} %reduce_sum.61, bf16[32,512]{1,0:T(8,128)(2,1)S(1)} %collective-permute-done, pred[]{:T(512)S(6)} %eq.7), kind=kOutput, calls=%fused_computation.37 | convolution fusion | flops 135168000 | bytes 2293761 | tf_op jit(solution)/shard_map/esh,ehd->esd/dot_general | solution.py:185
  120.5 0.4 collective-permute-start.1
  121.0 0.9 collective-permute-done.1
  121.9 33.3 %all_to_all.37 = bf16[32,32,512]{2,1,0:T(8,128)(2,1)S(1)} all-to-all(bf16[32,32,512]{2,1,0:T(8,128)(2,1)S(1)} %broadcast_in_dim.19), channel_id=1, replica_groups=mesh['frame'=8,'pos'=32] {'pos'}, dimensions={0} | all-to-all | bytes 2097152 | tf_op jit(solution)/shard_map/all_to_all | solution.py:16
  155.3 1.6 %fusion.17 = bf16[64,8,512]{2,1,0:T(8,128)(2,1)} fusion(bf16[1024,512]{1,0:T(8,128)(2,1)S(1)} %bitcast.114, bf16[512,512]{1,0:T(8,128)(2,1)S(1)} %copy-done.10, f32[512,1024]{1,0:T(8,128)S(1)} %copy-done.3, f32[512]{0:T(512)S(1)} %get-tuple-element.50, f32[512]{0:T(512)S(1)} %get-tuple-element.52), kind=kOutput, calls=%fused_computation.34 | convolution fusion | flops 539230208 | bytes 4198400 | tf_op jit(solution)/shard_map/dot_general | solution.py:202
  (71 shorter events, 3.7 us)
Async XLA Ops:
  0.0 54.3 %copy-start = (bf16[512,1024]{1,0:T(8,128)(2,1)S(1)}, bf16[512,1024]{1,0:T(8,128)(2,1)}, u32[]{:S(2)}) copy-start(bf16[512,1024]{1,0:T(8,128)(2,1)} %param.19) | copy-start | bytes 3145732
  0.0 18.1 %copy-start.5 = (bf16[512,512]{1,0:T(8,128)(2,1)S(1)}, bf16[512,512]{1,0:T(8,128)(2,1)}, u32[]{:S(2)}) copy-start(bf16[512,512]{1,0:T(8,128)(2,1)} %param.14) | copy-start | bytes 1572868
  0.0 19.4 %copy-start.6 = (bf16[512,512]{1,0:T(8,128)(2,1)S(1)}, bf16[512,512]{1,0:T(8,128)(2,1)}, u32[]{:S(2)}) copy-start(bf16[512,512]{1,0:T(8,128)(2,1)} %param.15) | copy-start | bytes 1572868
  3.5 14.6 %all-to-all-start = ((bf16[64,8,512]{2,0,1:T(8,128)(2,1)}), bf16[64,8,512]{2,0,1:T(8,128)(2,1)S(1)}, u32[]{:S(2)}, u32[]{:S(2)}) async-start(bf16[64,8,512]{2,0,1:T(8,128)(2,1)} %multiply_convert_fusion), calls=%async_computation | async-start | bytes 1048576 | tf_op jit(solution)/shard_map/all_to_all | solution.py:133
  18.1 1.8 %copy-start.7 = (bf16[512,512]{1,0:T(8,128)(2,1)S(1)}, bf16[512,512]{1,0:T(8,128)(2,1)}, u32[]{:S(2)}) copy-start(bf16[512,512]{1,0:T(8,128)(2,1)} %param.16) | copy-start | bytes 1572868
  34.5 9.6 %copy-start.1 = (bf16[64,8,512]{2,1,0:T(8,128)(2,1)S(1)}, bf16[64,8,512]{2,1,0:T(8,128)(2,1)}, u32[]{:S(2)}) copy-start(bf16[64,8,512]{2,1,0:T(8,128)(2,1)} %param.12) | copy-start | bytes 1572868
  40.4 11.8 %all-to-all-start.1 = ((bf16[8,64,1,512]{3,1,2,0:T(8,128)(2,1)}), bf16[8,64,1,512]{3,1,2,0:T(8,128)(2,1)S(1)}, u32[]{:S(2)}, u32[]{:S(2)}) async-start(bf16[8,64,1,512]{3,1,2,0:T(8,128)(2,1)} %constant_dynamic-update-slice_fusion), calls=%async_computation.1 | async-start | bytes 1048576 | tf_op jit(solution)/shard_map/all_to_all | solution.py:143
  44.1 10.2 %copy-start.8 = (f32[512]{0:T(512)S(1)}, f32[512]{0:T(512)}, u32[]{:S(2)}) copy-start(f32[512]{0:T(512)} %param.18) | copy-start | bytes 6148
  54.3 0.9 copy-start.9
  55.2 27.7 %copy-start.2 = (f32[512,1024]{1,0:T(8,128)}, f32[512,1024]{1,0:T(8,128)S(1)}, u32[]{:S(2)}) copy-start(f32[512,1024]{1,0:T(8,128)S(1)} %get-tuple-element.88) | copy-start | bytes 6291460
  84.8 34.0 %copy-start.4 = (bf16[1,1024,512]{2,1,0:T(8,128)(2,1)S(1)}, bf16[1,1024,512]{2,1,0:T(8,128)(2,1)}, u32[]{:S(2)}) copy-start(bf16[1,1024,512]{2,1,0:T(8,128)(2,1)} %param.21) | copy-start | bytes 3145732
  117.0 1.7 %collective-permute-start = (bf16[32,512]{1,0:T(8,128)(2,1)S(1)}, bf16[32,512]{1,0:T(8,128)(2,1)S(1)}, u32[]{:S(2)}, u32[]{:S(2)}) collective-permute-start(bf16[32,512]{1,0:T(8,128)(2,1)S(1)} %reduce_sum.61), channel_id=1, source_target_pairs={{0,1},{1,0},{2,3},{3,2},{4,5},{5,4},{6,7},{7,6},{8,9},{9,8},{10,11... | collective-permute-start | bytes 98312 | tf_op jit(solution)/shard_map/ppermute | solution.py:67
  120.5 34.8 %copy-start.3 = (f32[512,1024]{1,0:T(8,128)S(1)}, f32[512,1024]{1,0:T(8,128)}, u32[]{:S(2)}) copy-start(f32[512,1024]{1,0:T(8,128)} %copy-done.2) | copy-start | bytes 6291460
  120.5 34.8 %copy-start.10 = (bf16[512,512]{1,0:T(8,128)(2,1)S(1)}, bf16[512,512]{1,0:T(8,128)(2,1)}, u32[]{:S(2)}) copy-start(bf16[512,512]{1,0:T(8,128)(2,1)} %copy-done.9) | copy-start | bytes 1572868
  120.5 1.3 collective-permute-start.1
